TPU v7x, 128 devices: a whole 4x4x4 slice. The times are simulated.
128 devices in a mesh: row: 8 (over y, core), col: 16 (over x, z).
Axes of the slice: x: 4, y: 4, z: 4, core: 2. Of those that a mesh axis runs over, the one named last changes fastest.
Arguments:
- rhs_low: bfloat16 [32768, 512], P(('row', 'col')), may hold values from -6 to 6
- rhs_top: bfloat16 [16384, 512], P('row'), may hold values from -6 to 6
- lower_blocks: bfloat16 [128, 256, 128, 128], P('row', 'col'), may hold values from -0.03125 to 0.03125
- upper_blocks: bfloat16 [128, 256, 128, 128], P('row', 'col'), may hold values from -0.046875 to 0.046875
- block_target: int32 [128, 256], P('row', 'col'), may hold values from 0 to 15
- inv_lower_low: bfloat16 [256, 128, 128], P(('row', 'col')), as said below
- inv_upper_low: bfloat16 [256, 128, 128], P(('row', 'col')), as said below
- inv_lower_top: bfloat16 [128, 128, 128], P('row'), as said below
- inv_upper_top: bfloat16 [128, 128, 128], P('row'), as said below
Outputs:
- sol_low: bfloat16 [32768, 512], P(('row', 'col'))
- sol_top: bfloat16 [16384, 512], P(('row', 'col'))
Inputs may be any that keep to these rules, and one draw needn't show every extreme that they name: `inv_lower_low`: lower triangular with nonzero diagonal. `inv_upper_low`: upper triangular with nonzero diagonal. `inv_lower_top`: lower triangular with nonzero diagonal. `inv_upper_top`: upper triangular with nonzero diagonal.
All inputs are finite; a program needn't handle non-finite values.
Results may differ from a plain program's by a relative error of at most 0.024.
Values may be sent and summed in bfloat16 or wider, within the bound.
A program may use at most 128 MiB of HBM per device.

v0:
```python
import jax
import jax.numpy as jnp
from jax import lax
from jax.sharding import PartitionSpec as P


def body(
    rhs_low,
    rhs_top,
    lower_blocks,
    upper_blocks,
    block_target,
    inv_lower_low,
    inv_upper_low,
    inv_lower_top,
    inv_upper_top,
):
    width = inv_lower_low.shape[1]
    own_low = inv_lower_low.shape[0]
    rhs_count = rhs_low.shape[1]
    top_count = inv_lower_top.shape[0]
    own_top = top_count // lax.axis_size("col")
    rhs_blocks = rhs_low.reshape(own_low, width, rhs_count)
    fwd_low = jnp.einsum(
        "kab,kbj->kaj", inv_lower_low, rhs_blocks, preferred_element_type=jnp.float32
    ).astype(jnp.bfloat16)
    empty = jnp.zeros((top_count, width, rhs_count), jnp.float32)
    piece = lax.all_gather(fwd_low, "row", axis=0, tiled=True)
    blocks = lower_blocks
    targets = block_target

    def add_step(acc, item):
        blk, tgt = item
        prod = jnp.einsum("kab,kbj->kaj", blk, piece, preferred_element_type=jnp.float32)
        return (acc.at[tgt].add(prod), None)

    result, _ = lax.scan(add_step, empty, (blocks, targets))
    partial_top = result
    rhs_blocks_top = rhs_top.reshape(top_count, width, rhs_count)
    place = lax.axis_index("col") * own_top
    lsum = lax.psum_scatter(
        partial_top.astype(jnp.bfloat16), "col", scatter_dimension=0, tiled=True
    ).astype(jnp.float32)
    own_rhs = lax.dynamic_slice_in_dim(rhs_blocks_top, place, own_top, 0)
    own_lower = lax.dynamic_slice_in_dim(inv_lower_top, place, own_top, 0)
    own_upper = lax.dynamic_slice_in_dim(inv_upper_top, place, own_top, 0)
    resid_top = (own_rhs.astype(jnp.float32) - lsum).astype(jnp.bfloat16)
    fwd_top = jnp.einsum(
        "kab,kbj->kaj", own_lower, resid_top, preferred_element_type=jnp.float32
    ).astype(jnp.bfloat16)
    sol_top = jnp.einsum(
        "kab,kbj->kaj", own_upper, fwd_top, preferred_element_type=jnp.float32
    ).astype(jnp.bfloat16)
    solved_row = lax.all_gather(sol_top, "col", axis=0, tiled=True)
    blocks = upper_blocks
    targets = block_target

    def upper_step(acc, item):
        blk, tgt = item
        picked = jnp.take(solved_row, tgt, axis=0)
        return (
            acc + jnp.einsum("kab,kbj->kaj", blk, picked, preferred_element_type=jnp.float32),
            None,
        )

    begin = jnp.zeros((lax.axis_size("row") * own_low, width, rhs_count), jnp.float32)
    result, _ = lax.scan(upper_step, begin, (blocks, targets))
    usum = lax.psum_scatter(
        result.astype(jnp.bfloat16), "row", scatter_dimension=0, tiled=True
    ).astype(jnp.float32)
    resid_low = (fwd_low.astype(jnp.float32) - usum).astype(jnp.bfloat16)
    sol_low = jnp.einsum(
        "kab,kbj->kaj", inv_upper_low, resid_low, preferred_element_type=jnp.float32
    ).astype(jnp.bfloat16)
    return (
        sol_low.reshape(own_low * width, rhs_count),
        sol_top.reshape(own_top * width, rhs_count),
    )


def solution(mesh):
    placed = (
        P(("row", "col"), None),
        P("row", None),
        P("row", "col", None, None),
        P("row", "col", None, None),
        P("row", "col"),
        P(("row", "col"), None, None),
        P(("row", "col"), None, None),
        P("row", None, None),
        P("row", None, None),
    )
    return jax.shard_map(
        body,
        mesh=mesh,
        in_specs=placed,
        out_specs=(P(("row", "col"), None), P(("row", "col"), None)),
        check_vma=False,
    )
```

profile of v0, /device:TPU:0, one launch (start us, length us, event | category | flops | bytes accessed | tf_op | source)
XLA Modules:
  0.0 573.4 jit_solution(13332137533159201060)
XLA Ops:
  9.3 28.9 %all-gather.4.cloned.1.call-done = bf16[16,128,512]{2,1,0:T(8,128)(2,1)} async-done(((bf16[2,128,512]{2,1,0:T(8,128)(2,1)}), bf16[16,128,512]{2,1,0:T(8,128)(2,1)}) %all-gather.4.cloned.1.call-update) | async-done | bytes 2097168 | tf_op jit(solution)/shard_map/all_gather | solution.py:28
  38.1 2.5 broadcast.55
  40.6 220.8 %while.21 = (s32[]{:T(128)}, f32[16,128,512]{2,1,0:T(8,128)}, s32[16,16]{1,0:T(8,128)}, bf16[16,16,128,128]{3,2,1,0:T(8,128)(2,1)}, bf16[16,128,512]{2,1,0:T(8,128)(2,1)S(1)}, /*index=5*/s32[]{:T(128)}) while((s32[]{:T(128)}, f32[16,128,512]{2,1,0:T(8,128)}, s32[16,16]{1,0:T(8,128)}, bf16[16,16,128,128]{3,2,1,0:T(8,128)(2,1)}, ...), condition=%wide.region_2.3_spmd, body=%wide.region_0.2_spmd.sunk | while | flops 269484096 | bytes 19399432 | solution.py:37
  40.6 3.7 fusion.40
  45.0 9.5 %scatter_fusion = f32[16,128,512]{2,1,0:T(8,128)} fusion(f32[16,128,512]{2,1,0:T(8,128)} %get-tuple-element.165, s32[16]{0:T(128)S(1)} %fusion.39, f32[16,128,512]{2,1,0:T(8,128)} %fusion.40), kind=kCustom, calls=%fused_computation.1.clone.1 | custom fusion | flops 1048576 | bytes 12582976 | tf_op jit(solution)/shard_map/while/body/eval_jaxpr/scatter-add | solution.py:35
  54.5 3.7 fusion.40
  58.9 9.2 %scatter_fusion = f32[16,128,512]{2,1,0:T(8,128)} fusion(f32[16,128,512]{2,1,0:T(8,128)} %get-tuple-element.165, s32[16]{0:T(128)S(1)} %fusion.39, f32[16,128,512]{2,1,0:T(8,128)} %fusion.40), kind=kCustom, calls=%fused_computation.1.clone.1 | custom fusion | flops 1048576 | bytes 12582976 | tf_op jit(solution)/shard_map/while/body/eval_jaxpr/scatter-add | solution.py:35
  68.1 3.7 fusion.40
  72.5 9.4 %scatter_fusion = f32[16,128,512]{2,1,0:T(8,128)} fusion(f32[16,128,512]{2,1,0:T(8,128)} %get-tuple-element.165, s32[16]{0:T(128)S(1)} %fusion.39, f32[16,128,512]{2,1,0:T(8,128)} %fusion.40), kind=kCustom, calls=%fused_computation.1.clone.1 | custom fusion | flops 1048576 | bytes 12582976 | tf_op jit(solution)/shard_map/while/body/eval_jaxpr/scatter-add | solution.py:35
  81.9 3.7 fusion.40
  86.3 9.5 %scatter_fusion = f32[16,128,512]{2,1,0:T(8,128)} fusion(f32[16,128,512]{2,1,0:T(8,128)} %get-tuple-element.165, s32[16]{0:T(128)S(1)} %fusion.39, f32[16,128,512]{2,1,0:T(8,128)} %fusion.40), kind=kCustom, calls=%fused_computation.1.clone.1 | custom fusion | flops 1048576 | bytes 12582976 | tf_op jit(solution)/shard_map/while/body/eval_jaxpr/scatter-add | solution.py:35
  95.8 3.7 fusion.40
  100.1 9.3 %scatter_fusion = f32[16,128,512]{2,1,0:T(8,128)} fusion(f32[16,128,512]{2,1,0:T(8,128)} %get-tuple-element.165, s32[16]{0:T(128)S(1)} %fusion.39, f32[16,128,512]{2,1,0:T(8,128)} %fusion.40), kind=kCustom, calls=%fused_computation.1.clone.1 | custom fusion | flops 1048576 | bytes 12582976 | tf_op jit(solution)/shard_map/while/body/eval_jaxpr/scatter-add | solution.py:35
  109.5 3.7 fusion.40
  113.8 9.5 %scatter_fusion = f32[16,128,512]{2,1,0:T(8,128)} fusion(f32[16,128,512]{2,1,0:T(8,128)} %get-tuple-element.165, s32[16]{0:T(128)S(1)} %fusion.39, f32[16,128,512]{2,1,0:T(8,128)} %fusion.40), kind=kCustom, calls=%fused_computation.1.clone.1 | custom fusion | flops 1048576 | bytes 12582976 | tf_op jit(solution)/shard_map/while/body/eval_jaxpr/scatter-add | solution.py:35
  123.4 3.7 fusion.40
  127.7 9.5 %scatter_fusion = f32[16,128,512]{2,1,0:T(8,128)} fusion(f32[16,128,512]{2,1,0:T(8,128)} %get-tuple-element.165, s32[16]{0:T(128)S(1)} %fusion.39, f32[16,128,512]{2,1,0:T(8,128)} %fusion.40), kind=kCustom, calls=%fused_computation.1.clone.1 | custom fusion | flops 1048576 | bytes 12582976 | tf_op jit(solution)/shard_map/while/body/eval_jaxpr/scatter-add | solution.py:35
  137.2 3.7 fusion.40
  141.6 9.5 %scatter_fusion = f32[16,128,512]{2,1,0:T(8,128)} fusion(f32[16,128,512]{2,1,0:T(8,128)} %get-tuple-element.165, s32[16]{0:T(128)S(1)} %fusion.39, f32[16,128,512]{2,1,0:T(8,128)} %fusion.40), kind=kCustom, calls=%fused_computation.1.clone.1 | custom fusion | flops 1048576 | bytes 12582976 | tf_op jit(solution)/shard_map/while/body/eval_jaxpr/scatter-add | solution.py:35
  151.0 3.7 fusion.40
  155.4 9.2 %scatter_fusion = f32[16,128,512]{2,1,0:T(8,128)} fusion(f32[16,128,512]{2,1,0:T(8,128)} %get-tuple-element.165, s32[16]{0:T(128)S(1)} %fusion.39, f32[16,128,512]{2,1,0:T(8,128)} %fusion.40), kind=kCustom, calls=%fused_computation.1.clone.1 | custom fusion | flops 1048576 | bytes 12582976 | tf_op jit(solution)/shard_map/while/body/eval_jaxpr/scatter-add | solution.py:35
  164.6 3.7 fusion.40
  169.0 9.4 %scatter_fusion = f32[16,128,512]{2,1,0:T(8,128)} fusion(f32[16,128,512]{2,1,0:T(8,128)} %get-tuple-element.165, s32[16]{0:T(128)S(1)} %fusion.39, f32[16,128,512]{2,1,0:T(8,128)} %fusion.40), kind=kCustom, calls=%fused_computation.1.clone.1 | custom fusion | flops 1048576 | bytes 12582976 | tf_op jit(solution)/shard_map/while/body/eval_jaxpr/scatter-add | solution.py:35
  178.4 3.7 fusion.40
  182.8 9.4 %scatter_fusion = f32[16,128,512]{2,1,0:T(8,128)} fusion(f32[16,128,512]{2,1,0:T(8,128)} %get-tuple-element.165, s32[16]{0:T(128)S(1)} %fusion.39, f32[16,128,512]{2,1,0:T(8,128)} %fusion.40), kind=kCustom, calls=%fused_computation.1.clone.1 | custom fusion | flops 1048576 | bytes 12582976 | tf_op jit(solution)/shard_map/while/body/eval_jaxpr/scatter-add | solution.py:35
  192.1 3.7 fusion.40
  196.5 9.4 %scatter_fusion = f32[16,128,512]{2,1,0:T(8,128)} fusion(f32[16,128,512]{2,1,0:T(8,128)} %get-tuple-element.165, s32[16]{0:T(128)S(1)} %fusion.39, f32[16,128,512]{2,1,0:T(8,128)} %fusion.40), kind=kCustom, calls=%fused_computation.1.clone.1 | custom fusion | flops 1048576 | bytes 12582976 | tf_op jit(solution)/shard_map/while/body/eval_jaxpr/scatter-add | solution.py:35
  205.9 3.7 fusion.40
  210.3 9.6 %scatter_fusion = f32[16,128,512]{2,1,0:T(8,128)} fusion(f32[16,128,512]{2,1,0:T(8,128)} %get-tuple-element.165, s32[16]{0:T(128)S(1)} %fusion.39, f32[16,128,512]{2,1,0:T(8,128)} %fusion.40), kind=kCustom, calls=%fused_computation.1.clone.1 | custom fusion | flops 1048576 | bytes 12582976 | tf_op jit(solution)/shard_map/while/body/eval_jaxpr/scatter-add | solution.py:35
  219.9 3.7 fusion.40
  224.3 9.4 %scatter_fusion = f32[16,128,512]{2,1,0:T(8,128)} fusion(f32[16,128,512]{2,1,0:T(8,128)} %get-tuple-element.165, s32[16]{0:T(128)S(1)} %fusion.39, f32[16,128,512]{2,1,0:T(8,128)} %fusion.40), kind=kCustom, calls=%fused_computation.1.clone.1 | custom fusion | flops 1048576 | bytes 12582976 | tf_op jit(solution)/shard_map/while/body/eval_jaxpr/scatter-add | solution.py:35
  233.7 3.7 fusion.40
  238.1 9.5 %scatter_fusion = f32[16,128,512]{2,1,0:T(8,128)} fusion(f32[16,128,512]{2,1,0:T(8,128)} %get-tuple-element.165, s32[16]{0:T(128)S(1)} %fusion.39, f32[16,128,512]{2,1,0:T(8,128)} %fusion.40), kind=kCustom, calls=%fused_computation.1.clone.1 | custom fusion | flops 1048576 | bytes 12582976 | tf_op jit(solution)/shard_map/while/body/eval_jaxpr/scatter-add | solution.py:35
  247.6 3.7 fusion.40
  251.9 9.4 %scatter_fusion = f32[16,128,512]{2,1,0:T(8,128)} fusion(f32[16,128,512]{2,1,0:T(8,128)} %get-tuple-element.165, s32[16]{0:T(128)S(1)} %fusion.39, f32[16,128,512]{2,1,0:T(8,128)} %fusion.40), kind=kCustom, calls=%fused_computation.1.clone.1 | custom fusion | flops 1048576 | bytes 12582976 | tf_op jit(solution)/shard_map/while/body/eval_jaxpr/scatter-add | solution.py:35
  261.4 3.8 convert_element_type.46
  265.3 76.5 %reduce-scatter.7.cloned.1.call-done = bf16[1,128,512]{2,1,0:T(8,128)(2,1)} async-done(((bf16[16,128,512]{2,1,0:T(8,128)(2,1)}), bf16[1,128,512]{2,1,0:T(8,128)(2,1)}) %reduce-scatter.7.cloned.1.call-update) | async-done | bytes 131088
  343.9 45.0 %all-gather.6.cloned.1.call-done = bf16[2048,512]{1,0:T(8,128)(2,1)} async-done(((bf16[128,512]{1,0:T(8,128)(2,1)}), bf16[2048,512]{1,0:T(8,128)(2,1)}) %all-gather.6.cloned.1.call-update) | async-done | bytes 2097168 | tf_op jit(solution)/shard_map/all_gather | solution.py:54
  388.9 139.0 %while.22 = (s32[]{:T(128)}, f32[16,128,512]{2,1,0:T(8,128)}, bf16[16,16,128,128]{3,2,1,0:T(8,128)(2,1)}, s32[16,16]{1,0:T(8,128)}, bf16[16,128,512]{2,1,0:T(8,128)(2,1)}, /*index=5*/s32[]{:T(128)}, s32[]{:T(128)}) while((s32[]{:T(128)}, f32[16,128,512]{2,1,0:T(8,128)}, bf16[16,16,128,128]{3,2,1,0:T(8,128)(2,1)}, ...), condition=%wide.region_5.6_spmd.clone, body=%wide.region_4.5_spmd.clone.sunk | while | flops 271582368 | bytes 15209407 | solution.py:67
  389.6 2.3 gather_fusion
  392.5 3.8 select_add_fusion.2
  397.0 2.3 gather_fusion
  400.0 5.1 select_add_fusion.2
  408.8 5.1 select_add_fusion.2
  417.5 5.1 select_add_fusion.2
  426.3 5.1 select_add_fusion.2
  435.1 5.1 select_add_fusion.2
  440.9 2.3 gather_fusion
  443.9 5.1 select_add_fusion.2
  449.6 2.3 gather_fusion
  452.6 5.1 select_add_fusion.2
  461.4 5.1 select_add_fusion.2
  470.2 5.1 select_add_fusion.2
  478.9 5.1 select_add_fusion.2
  487.7 5.1 select_add_fusion.2
  493.5 2.3 gather_fusion
  496.5 5.1 select_add_fusion.2
  502.3 2.3 gather_fusion
  505.3 5.1 select_add_fusion.2
  511.1 2.3 gather_fusion
  514.0 5.1 select_add_fusion.2
  522.8 5.1 select_add_fusion.2
  527.9 3.8 convert_element_type.52
  531.8 33.2 %reduce-scatter.5.cloned.1.call-done = bf16[2,128,512]{2,1,0:T(8,128)(2,1)} async-done(((bf16[16,128,512]{2,1,0:T(8,128)(2,1)}), bf16[2,128,512]{2,1,0:T(8,128)(2,1)}) %reduce-scatter.5.cloned.1.call-update) | async-done | bytes 262160 | tf_op jit(solution)/shard_map/reduce_scatter | solution.py:68
  (93 shorter events, 60.1 us)
Async XLA Ops:
  7.2 334.6 %copy-start = (bf16[16,128,128]{2,1,0:T(8,128)(2,1)S(1)}, bf16[16,128,128]{2,1,0:T(8,128)(2,1)}, u32[]{:S(2)}) copy-start(bf16[16,128,128]{2,1,0:T(8,128)(2,1)} %param.20) | copy-start | bytes 1572868
  7.2 30.9 %all-gather.4.cloned.1.call-start = ((), (), s32[]{:S(2)}) async-start(), calls=%async_computation.2 | async-start | bytes 2359296 | tf_op jit(solution)/shard_map/all_gather | solution.py:28
  9.2 332.6 %reduce-scatter.7.cloned.1.call-start = ((), (), s32[]{:S(2)}) async-start(), calls=%async_computation.5 | async-start | bytes 2228224
  38.1 2.5 copy-start.1
  265.2 123.6 %all-gather.6.cloned.1.call-start = ((), (), s32[]{:S(2)}) async-start(), calls=%async_computation.4 | async-start | bytes 2228224 | tf_op jit(solution)/shard_map/all_gather | solution.py:54
  343.8 221.2 %reduce-scatter.5.cloned.1.call-start = ((), (), s32[]{:S(2)}) async-start(), calls=%async_computation.3 | async-start | bytes 2359296 | tf_op jit(solution)/shard_map/reduce_scatter | solution.py:68
  527.9 37.1 %copy-start.2 = (bf16[2,128,512]{2,1,0:T(8,128)(2,1)S(1)}, bf16[2,128,512]{2,1,0:T(8,128)(2,1)}, u32[]{:S(2)}) copy-start(bf16[2,128,512]{2,1,0:T(8,128)(2,1)} %convolution_convert_fusion.1) | copy-start | bytes 786436
  527.9 37.1 %copy-start.3 = (bf16[2,128,128]{2,1,0:T(8,128)(2,1)S(1)}, bf16[2,128,128]{2,1,0:T(8,128)(2,1)}, u32[]{:S(2)}) copy-start(bf16[2,128,128]{2,1,0:T(8,128)(2,1)} %param.19) | copy-start | bytes 196612
Sparse Core Ops, SparseCore 0:
  10.3 27.7 all-gather.3
  265.3 76.4 reduce-scatter.6
  344.5 44.2 all-gather.5
  531.9 33.0 reduce-scatter.4
where the time goes:
time: 577 us; the launch traced here: 573 us
  other arithmetic  192 us (33%)
  waiting for transfers between devices  184 us (32%)
  matrix products  145 us (25%)
  local copies, waits for them, and re-layouts  38.9 us (7%)
  between operations  13.8 us (2%)
    scatter-add x16, other arithmetic, add_step(): return (acc.at[tgt].add(prod), None)  151 us
    dot_general x16, matrix products, upper_step(): jnp.einsum('kab,kbj->kaj', blk, picked, preferred_element_type=jnp.float32)  80.1 us
    unnamed x5, waiting for transfers between devices  76.6 us
    dot_general x16, matrix products, add_step(): jnp.einsum('kab,kbj->kaj', blk, piece, preferred_element_type=jnp.float32)  58.9 us
    all_gather x1, waiting for transfers between devices, body(): solved_row = lax.all_gather(sol_top, 'col', axis=0, tiled=True)  45 us
    gather x16, local copies, waits for them, and re-layouts, upper_step(): picked = jnp.take(solved_row, tgt, axis=0)  36.3 us
    reduce_scatter x1, waiting for transfers between devices, body(): lax.psum_scatter(result.astype(jnp.bfloat16), 'row', scatter_dimension=0,...  33.2 us
    all_gather x1, waiting for transfers between devices, body(): piece = lax.all_gather(fwd_low, 'row', axis=0, tiled=True)  28.9 us
  transfers between devices with their start and end apart: 4, of which 4 were waited for; matrix products, arithmetic and copies ran while one was open for 0% of the time, Pallas kernels for 0%

commit v1 on v0

v1 whole, which is shorter than its diff:
```python
import functools

import jax
import jax.numpy as jnp
from jax import lax
from jax.experimental import pallas as pl
from jax.experimental.pallas import tpu as pltpu
from jax.sharding import PartitionSpec as P

RING = 4
CHUNKS = 2
BF, F32 = jnp.bfloat16, jnp.float32
MESH = pl.DeviceIdType.MESH


def wrap(i):
    return lax.rem(i + RING, RING)


def dot(a, b):
    return jnp.dot(a, b, preferred_element_type=F32)


def kernel(
    names,
    tbl,
    rhs_low,
    rhs_top,
    lower,
    upper,
    inv_ll,
    inv_ul,
    inv_lt,
    inv_ut,
    out_low,
    out_top,
    *scratch,
):
    s = dict(zip(names, scratch))
    slots, positions, B, _ = lower.shape
    n = s["fwd"].shape[2]
    half = B // 2
    r, c = lax.axis_index("row"), lax.axis_index("col")
    y, core = lax.div(r, 2), lax.rem(r, 2)
    x, z = lax.div(c, RING), lax.rem(c, RING)
    partner = (y * 2 + 1 - core, c)

    def y_at(d):
        return (wrap(y + d) * 2 + core, c)

    def x_at(d):
        return (r, wrap(x + d) * RING + z)

    def z_at(d):
        return (r, x * RING + wrap(z + d))

    barrier = pltpu.get_barrier_semaphore()
    neighbours = [partner] + [at(d) for at in (y_at, x_at, z_at) for d in (1, -1)]
    for device in neighbours:
        pl.semaphore_signal(barrier, inc=1, device_id=device, device_id_type=MESH)

    local_count = [0]
    local_open = []

    def local(src, dst):
        copy = pltpu.make_async_copy(src, dst, s["local_sem"].at[local_count[0]])
        local_count[0] += 1
        copy.start()
        return copy

    small = [
        local(rhs_low, s["rhs_low"]),
        local(inv_ll, s["inv_ll"]),
    ]
    group = positions // 4
    lower_in = [
        local(lower.at[:, pl.ds(g * group, group)], s["low_in"].at[:, pl.ds(g * group, group)])
        for g in range(4)
    ]
    top_in = [
        local(rhs_top.at[pl.ds(pl.multiple_of(c * B, B), B)], s["rhs_top"]),
        local(inv_lt.at[c], s["inv_lt"]),
        local(inv_ut.at[c], s["inv_ut"]),
        local(inv_ul, s["inv_ul"]),
    ]
    upper_in = [
        local(upper.at[:, pl.ds(g * group, group)], s["up_in"].at[:, pl.ds(g * group, group)])
        for g in range(4)
    ]

    remote_ids = {}
    sends = []

    def remote_id(key):
        return remote_ids.setdefault(key, len(remote_ids))

    def send(key, src, dst, device):
        i = remote_id(key)
        copy = pltpu.make_async_remote_copy(
            src_ref=src,
            dst_ref=dst,
            send_sem=s["send_sem"].at[i],
            recv_sem=s["recv_sem"].at[i],
            device_id=device,
            device_id_type=MESH,
        )
        copy.start()
        sends.append(copy)

    def arrive(key, dst):
        i = remote_id(key)
        pltpu.make_async_remote_copy(
            src_ref=dst,
            dst_ref=dst,
            send_sem=s["send_sem"].at[i],
            recv_sem=s["recv_sem"].at[i],
            device_id=partner,
            device_id_type=MESH,
        ).wait_recv()

    for copy in small:
        copy.wait()

    def own_rows(row):
        return pl.ds(pl.multiple_of(row * (2 * B), 2 * B), 2 * B)

    def own_half(row, j):
        return pl.ds(pl.multiple_of(row * (2 * B) + j * B, B), B)

    for j in range(2):
        solved = dot(s["inv_ll"][j], s["rhs_low"][pl.ds(j * B, B)]).astype(BF)
        for k in range(CHUNKS):
            s["fwd"][k, own_half(r, j)] = solved[:, k * n : (k + 1) * n]

    pl.semaphore_wait(barrier, len(neighbours))

    s["sum_a"][0] = jnp.zeros((B, B), F32)
    s["sum_b"][0] = jnp.zeros((B, B), F32)

    def build(source, arrivals, write):
        hop = positions // 2
        pending = list(arrivals)

        def one(acc, m):
            for e in range(slots):
                before = tbl[e * positions + m]
                acc[e + 1] = source[e, m].astype(F32) + acc[before]

        def put(acc, m):
            for q in range(slots):
                last = tbl[(slots + q) * positions + m]
                write(q, m, acc[last].astype(BF))

        def step(i, carry):
            m0, m1 = 2 * i, 2 * i + 1
            one(s["sum_a"], m0)
            one(s["sum_b"], m1)
            put(s["sum_a"], m0)
            put(s["sum_b"], m1)
            return carry

        per = group // 2
        for g in range(4):
            pending[g].wait()
            lax.fori_loop(g * per, (g + 1) * per, step, 0)
            yield

    def write_low(q, m, value):
        s["low"][q // RING, q % RING, :, pl.ds(pl.multiple_of(m * B, B), B)] = value

    def write_up(q, m, value):
        s["up"][m, :, pl.ds(q * B, B)] = value

    low_build = build(s["low_in"], lower_in, write_low)
    up_build = build(s["up_in"], upper_in, write_up)

    def builds():
        yield from low_build
        yield from up_build

    building = builds()

    def finish(gen):
        for _ in gen:
            pass

    def reduce_ring(tag, k, at, piece, name):
        s1, r1 = s[name + "_s1"].at[k], s[name + "_r1"].at[k]
        s2, r2 = s[name + "_s2"].at[k], s[name + "_r2"].at[k]
        acc = s[name + "_acc"].at[k]
        s1[...] = piece(2).astype(BF)
        send((tag, "far", 1), s1.at[0], r1.at[0], at(1))
        send((tag, "far", -1), s1.at[1], r1.at[1], at(-1))
        acc[0] = piece(1)
        s2[0, 1] = acc[0, 1].astype(BF)
        send((tag, "near", 1), s2.at[0, 1], r2.at[0, 1], at(1))
        acc[1] = piece(-1)
        s2[1, 0] = acc[1, 0].astype(BF)
        send((tag, "near", -1), s2.at[1, 0], r2.at[1, 0], at(-1))
        acc[2] = piece(0)
        yield
        arrive((tag, "far", 1), r1.at[0])
        s2[0, 0] = (acc[0, 0] + r1[0].astype(F32)).astype(BF)
        send((tag, "sum", 1), s2.at[0, 0], r2.at[0, 0], at(1))
        arrive((tag, "far", -1), r1.at[1])
        s2[1, 1] = (acc[1, 1] + r1[1].astype(F32)).astype(BF)
        send((tag, "sum", -1), s2.at[1, 1], r2.at[1, 1], at(-1))
        yield
        for step, d, h in (("near", 1, 1), ("near", -1, 0), ("sum", 1, 0), ("sum", -1, 1)):
            arrive((tag, step, d), r2.at[0 if d == 1 else 1, h])
        acc[2] = acc[2] + r2[0].astype(F32) + r2[1].astype(F32)

    def chunk(k):
        heavy_x = k % 2 == 0
        heavy_at, light_at = (x_at, z_at) if heavy_x else (z_at, x_at)
        h, l = (x, z) if heavy_x else (z, x)
        fwd, solved = s["fwd"].at[k], s["solved"].at[k]

        def row_of(d, side):
            return wrap(y + d) * 2 + (core if side == 0 else 1 - core)

        own = fwd.at[own_rows(r)]
        send((k, "gy", 1), own, own, y_at(1))
        send((k, "gy", -1), own, own, y_at(-1))
        send((k, "gc", 0), own, own, partner)
        yield
        before = fwd.at[own_rows(row_of(-1, 0))]
        arrive((k, "gy", 1), before)
        part = fwd.at[own_half(row_of(-1, 0), 0)]
        send((k, "gy2", 1), part, part, y_at(1))
        send((k, "gc", -1), before, before, partner)
        after = fwd.at[own_rows(row_of(1, 0))]
        arrive((k, "gy", -1), after)
        part = fwd.at[own_half(row_of(1, 0), 1)]
        send((k, "gy2", -1), part, part, y_at(-1))
        send((k, "gc", 1), after, after, partner)
        yield
        for j, d in ((0, 1), (1, -1)):
            part = fwd.at[own_half(row_of(2, 0), j)]
            arrive((k, "gy2", d), part)
            send((k, "gc2", j), part, part, partner)
        yield
        finish(low_build)
        for d in (0, -1, 1):
            arrive((k, "gc", d), fwd.at[own_rows(row_of(d, 1))])
        for j in range(2):
            arrive((k, "gc2", j), fwd.at[own_half(row_of(2, 1), j)])

        def top_piece(d):
            p = wrap(h + d)
            rows = s["low"][p] if heavy_x else s["low"][:, p]
            return dot(rows.reshape(RING * B, -1), fwd[...]).reshape(2, 2 * B, n)

        yield from reduce_ring((k, "heavy"), k, heavy_at, top_piece, "heavy")
        summed = s["heavy_acc"]

        def light_piece(d):
            p = wrap(l + d)
            q, t = lax.div(p, 2), lax.rem(p, 2)
            start = pl.multiple_of(t * B, B)
            return summed[k, 2, q, pl.ds(start, B)].reshape(2, half, n)

        yield from reduce_ring((k, "light"), k, light_at, light_piece, "light")
        lsum = s["light_acc"][k, 2].reshape(B, n)

        if k == 0:
            for copy in top_in:
                copy.wait()
        resid_top = (s["rhs_top"][:, k * n : (k + 1) * n].astype(F32) - lsum).astype(BF)
        fwd_top = dot(s["inv_lt"][...], resid_top).astype(BF)
        solved[x, z] = dot(s["inv_ut"][...], fwd_top).astype(BF)
        local_open.append(local(solved.at[x, z], out_top.at[:, pl.ds(k * n, n)]))

        def block(dh, dl):
            a, b = wrap(h + dh), wrap(l + dl)
            return solved.at[a, b] if heavy_x else solved.at[b, a]

        def part_of(ref, i):
            return ref.at[pl.ds(i * half, half)]

        def spread(dl):
            for d in (1, -1):
                send((k, "sh", dl, d), block(0, dl), block(0, dl), heavy_at(d))

        for d in (1, -1):
            send((k, "sl", d), block(0, 0), block(0, 0), light_at(d))
        spread(0)
        yield
        arrive((k, "sl", 1), block(0, -1))
        part = part_of(block(0, -1), 0)
        send((k, "sl2", 1), part, part, light_at(1))
        spread(-1)
        arrive((k, "sl", -1), block(0, 1))
        part = part_of(block(0, 1), 1)
        send((k, "sl2", -1), part, part, light_at(-1))
        spread(1)
        yield
        arrive((k, "sl2", 1), part_of(block(0, 2), 0))
        arrive((k, "sl2", -1), part_of(block(0, 2), 1))
        spread(2)
        for dl in (0, 1):
            arrive((k, "sh", dl, 1), block(-1, dl))
            send((k, "sh2", dl), block(-1, dl), block(-1, dl), heavy_at(1))
        arrive((k, "sh", -1, -1), block(1, -1))
        send((k, "sh2", -1), block(1, -1), block(1, -1), heavy_at(-1))
        yield
        arrive((k, "sh", 2, -1), block(1, 2))
        send((k, "sh2", 2), block(1, 2), block(1, 2), heavy_at(-1))
        yield
        finish(low_build)
        finish(up_build)
        for dl in (-1, 2):
            arrive((k, "sh", dl, 1), block(-1, dl))
        for dl in (0, 1):
            arrive((k, "sh", dl, -1), block(1, dl))
        for dl in (0, 1, -1, 2):
            arrive((k, "sh2", dl), block(2, dl))

        def low_rows(d, side):
            first = pl.multiple_of(row_of(d, side) * 2, 2)
            rows = s["up"][pl.ds(first, 2)].reshape(2 * B, -1)
            return dot(rows, solved[...].reshape(-1, n))

        for d in (2, 1, -1, 0):
            i = d % RING
            s["pair_s"][k, i] = low_rows(d, 1).astype(BF)
            send((k, "pair", d), s["pair_s"].at[k, i], s["pair_r"].at[k, i], partner)
        yield

        def low_piece(d):
            mine = low_rows(d, 0)
            arrive((k, "pair", d), s["pair_r"].at[k, d % RING])
            return (mine + s["pair_r"][k, d % RING].astype(F32)).reshape(2, B, n)

        yield from reduce_ring((k, "low"), k, y_at, low_piece, "row")
        usum = s["row_acc"].at[k, 2]
        for j in range(2):
            resid = (fwd[own_half(r, j)].astype(F32) - usum[j]).astype(BF)
            s["out_low"][k, pl.ds(j * B, B)] = dot(s["inv_ul"][j], resid).astype(BF)
        local_open.append(local(s["out_low"].at[k], out_low.at[:, pl.ds(k * n, n)]))

    live = [chunk(k) for k in range(CHUNKS)]
    while live:
        for gen in list(live):
            if next(gen, "done") == "done":
                live.remove(gen)
            next(building, None)
    for copy in local_open:
        copy.wait()
    for copy in sends:
        copy.wait_send()


def tables(targets):
    slots = targets.shape[0]
    order = jnp.arange(slots, dtype=jnp.int32)
    number = (order + 1)[:, None, None]
    same = targets[:, None, :] == targets[None, :, :]
    earlier = (order[:, None] < order[None, :])[:, :, None]
    before = jnp.max(jnp.where(same & earlier, number, 0), axis=0)
    hit = targets[:, None, :] == order[None, :, None]
    last = jnp.max(jnp.where(hit, number, 0), axis=0)
    return jnp.concatenate([before, last], axis=0).reshape(-1)


def body(
    rhs_low,
    rhs_top,
    lower_blocks,
    upper_blocks,
    block_target,
    inv_lower_low,
    inv_upper_low,
    inv_lower_top,
    inv_upper_top,
):
    slots, positions, B, _ = lower_blocks.shape
    count = rhs_low.shape[1]
    C, n = CHUNKS, rhs_low.shape[1] // CHUNKS
    VM = pltpu.VMEM

    def ring(name, depth):
        return {
            name + "_s1": VM((C, 2, depth, n), BF),
            name + "_r1": VM((C, 2, depth, n), BF),
            name + "_s2": VM((C, 2, 2, depth, n), BF),
            name + "_r2": VM((C, 2, 2, depth, n), BF),
            name + "_acc": VM((C, 3, 2, depth, n), F32),
        }

    scratch = {
        "rhs_low": VM(rhs_low.shape, BF),
        "inv_ll": VM(inv_lower_low.shape, BF),
        "inv_ul": VM(inv_upper_low.shape, BF),
        "rhs_top": VM((B, count), BF),
        "inv_lt": VM((B, B), BF),
        "inv_ut": VM((B, B), BF),
        "low_in": VM(lower_blocks.shape, BF),
        "up_in": VM(upper_blocks.shape, BF),
        "low": VM((RING, RING, B, positions * B), BF),
        "up": VM((positions, B, RING * RING * B), BF),
        "sum_a": VM((slots + 1, B, B), F32),
        "sum_b": VM((slots + 1, B, B), F32),
        "fwd": VM((C, positions * B, n), BF),
        "solved": VM((C, RING, RING, B, n), BF),
        "pair_s": VM((C, RING, 2 * B, n), BF),
        "pair_r": VM((C, RING, 2 * B, n), BF),
        "out_low": VM((C, 2 * B, n), BF),
        **ring("heavy", 2 * B),
        **ring("light", B // 2),
        **ring("row", B),
        "local_sem": pltpu.SemaphoreType.DMA((14 + 2 * C,)),
        "send_sem": pltpu.SemaphoreType.DMA((50 * C,)),
        "recv_sem": pltpu.SemaphoreType.DMA((50 * C,)),
    }
    anywhere = pl.BlockSpec(memory_space=pl.ANY)
    return pl.pallas_call(
        functools.partial(kernel, tuple(scratch)),
        out_shape=(
            jax.ShapeDtypeStruct((2 * B, count), BF),
            jax.ShapeDtypeStruct((B, count), BF),
        ),
        in_specs=[pl.BlockSpec(memory_space=pltpu.SMEM)] + [anywhere] * 8,
        out_specs=(anywhere, anywhere),
        scratch_shapes=list(scratch.values()),
        compiler_params=pltpu.CompilerParams(
            collective_id=0, has_side_effects=True, vmem_limit_bytes=66_000_000
        ),
    )(
        tables(block_target),
        rhs_low,
        rhs_top,
        lower_blocks,
        upper_blocks,
        inv_lower_low,
        inv_upper_low,
        inv_lower_top,
        inv_upper_top,
    )


def solution(mesh):
    placed = (
        P(("row", "col"), None),
        P("row", None),
        P("row", "col", None, None),
        P("row", "col", None, None),
        P("row", "col"),
        P(("row", "col"), None, None),
        P(("row", "col"), None, None),
        P("row", None, None),
        P("row", None, None),
    )
    return jax.shard_map(
        body,
        mesh=mesh,
        in_specs=placed,
        out_specs=(P(("row", "col"), None), P(("row", "col"), None)),
        check_vma=False,
    )
```

time: 577 us -> 83.4 us (0.14)
  other arithmetic: 192 us -> 0.91 us
  waiting for transfers between devices: 184 us -> 0 us
  matrix products: 145 us -> 0 us
  Pallas kernels: 0 us -> 77.2 us
  local copies, waits for them, and re-layouts: 38.9 us -> 3.9 us
  between operations: 13.8 us -> 0.67 us
    scatter-add x16 -> x0, other arithmetic: 151 us -> none  [add_step(): return (acc.at[tgt].add(prod), None)]
    dot_general x35 -> x0, matrix products: 145 us -> none  [the longest x16 80.1 us: upper_step(): jnp.einsum('kab,kbj->kaj', blk, picked, preferred_element_type=jnp.float32)]
    pallas_call x0 -> x1, Pallas kernels: none -> 77.2 us  [body(): pl.pallas_call(functools.partial(kernel, tuple(scratch)), out_shape=(jax....]
    unnamed x5 -> x0, waiting for transfers between devices: 76.6 us -> none
    all_gather x2 -> x0, waiting for transfers between devices: 73.8 us -> none  [the longest x1 45 us: body(): solved_row = lax.all_gather(sol_top, 'col', axis=0, tiled=True)]
    gather x16 -> x0, local copies, waits for them, and re-layouts: 36.3 us -> none  [upper_step(): picked = jnp.take(solved_row, tgt, axis=0)]
    reduce_scatter x1 -> x0, waiting for transfers between devices: 33.2 us -> none  [body(): lax.psum_scatter(result.astype(jnp.bfloat16), 'row', scatter_dimension=0,...]
    select_n x32 -> x0, other arithmetic: 22.2 us -> none  [the longest x16 11.1 us: add_step(): return (acc.at[tgt].add(prod), None)]
  transfers between devices with their start and end apart: 4 -> 0, of which waited for: 4 -> 0; matrix products, arithmetic and copies ran while one was open for 0% -> 0% of each run, Pallas kernels for 0% -> 0%
where the time goes in v1:
time: 83.4 us; the launch traced here: 82.7 us
  Pallas kernels  77.2 us (93%)
  local copies, waits for them, and re-layouts  3.9 us (5%)
  other arithmetic  0.91 us (1%)
    pallas_call x1, Pallas kernels, body(): pl.pallas_call(functools.partial(kernel, tuple(scratch)), out_shape=(jax....  77.2 us
    unnamed x2, local copies, waits for them, and re-layouts  3.24 us

profile of v1, /device:TPU:0, one launch (start us, length us, event | category | flops | bytes accessed | tf_op | source)
XLA Modules:
  0.0 82.7 jit_solution(6429744986672939425)
XLA Ops:
  0.7 0.9 %select_reduce_fusion.1 = (s32[16,16]{1,0:T(8,128)S(1)}, s32[16,16]{1,0:T(8,128)S(1)}) fusion(s32[16]{0:T(128)S(1)} %iota_add_fusion, s32[16,16]{1,0:T(8,128)} %param.13, pred[16,16]{1,0:T(8,128)(4,1)S(1)} %iota_compare_fusion.1), kind=kLoop, calls=%fused_computation.2 | loop fusion | flops 28160 | bytes 3392 | tf_op jit(solution)/shard_map/reduce_max | solution.py:360
  1.6 0.7 reshape.25.tbl
  2.2 77.2 %shard_map.104 = (bf16[256,512]{1,0:T(8,128)(2,1)}, bf16[128,512]{1,0:T(8,128)(2,1)}) custom-call(s32[512]{0:T(512)} %reshape.25.tbl, bf16[256,512]{1,0:T(8,128)(2,1)} %rhs_low.1, bf16[2048,512]{1,0:T(8,128)(2,1)} %rhs_top.1, bf16[16,16,128,128]{3,2,1,0:T(8,128)(2,1)} %lower.1, bf16[16,16,128,128]{3,2,1,0:T(8,128)(2,1)} %upper.1, ...), custom_call_target="tpu_custom_call" | custom-call | tf_op jit(solution)/shard_map/pallas_call | solution.py:417
  79.5 1.7 %copy.13 = bf16[256,512]{1,0:T(8,128)(2,1)} copy(bf16[256,512]{1,0:T(8,128)(2,1)} %get-tuple-element.6) | data formatting | bytes 524288
  81.2 1.6 %copy.14 = bf16[128,512]{1,0:T(8,128)(2,1)} copy(bf16[128,512]{1,0:T(8,128)(2,1)} %get-tuple-element.7) | data formatting | bytes 262144
  (3 shorter events, 0.0 us)

commit v2 on v1

v2 whole, which is shorter than its diff:
```python
import functools
import math

import jax
import jax.numpy as jnp
from jax import lax
from jax.experimental import pallas as pl
from jax.experimental.pallas import tpu as pltpu
from jax.sharding import PartitionSpec as P

RING = 4
NEAR_FIRST = (0, -1, 1, 2)
LIGHT = (1, -1, 2)
GROUPS = 2
LAG = 0
BF, F32 = jnp.bfloat16, jnp.float32
MESH = pl.DeviceIdType.MESH


def wrap(i):
    return lax.rem(i + RING, RING)


def dot(a, b):
    return jnp.dot(a, b, preferred_element_type=F32)


def kernel(
    names,
    target,
    rhs_low,
    rhs_top,
    lower,
    upper,
    inv_ll,
    inv_ul,
    inv_lt,
    inv_ut,
    out_low,
    out_top,
    *scratch,
):
    s = dict(zip(names, scratch))
    slots, positions, B, _ = lower.shape
    n = s["fwd"].shape[2]
    w = n // 2
    r, c = lax.axis_index("row"), lax.axis_index("col")
    y, core = lax.div(r, 2), lax.rem(r, 2)
    x, z = lax.div(c, RING), lax.rem(c, RING)
    partner = (y * 2 + 1 - core, c)

    def y_at(d):
        return (wrap(y + d) * 2 + core, c)

    def x_at(d):
        return (r, wrap(x + d) * RING + z)

    def z_at(d):
        return (r, x * RING + wrap(z + d))

    barrier = pltpu.get_barrier_semaphore()
    neighbours = [partner] + [at(d) for at in (y_at, x_at, z_at) for d in (1, -1)]
    for device in neighbours:
        pl.semaphore_signal(barrier, inc=1, device_id=device, device_id_type=MESH)

    local_count = [0]
    local_open = []

    def local(src, dst):
        copy = pltpu.make_async_copy(src, dst, s["local_sem"].at[local_count[0]])
        local_count[0] += 1
        copy.start()
        return copy

    small = [
        local(rhs_low, s["rhs_low"]),
        local(inv_ll, s["inv_ll"]),
        local(target, s["target"]),
    ]
    quarter = positions // 4
    lower_in = []
    for d in NEAR_FIRST:
        mine = pl.ds(pl.multiple_of(wrap(y + d) * quarter, quarter), quarter)
        lower_in.append(local(lower.at[:, mine], s["low_in"].at[:, mine]))
    top_in = [
        local(rhs_top.at[pl.ds(pl.multiple_of(c * B, B), B)], s["rhs_top"]),
        local(inv_lt.at[c], s["inv_lt"]),
        local(inv_ut.at[c], s["inv_ut"]),
        local(inv_ul, s["inv_ul"]),
    ]
    upper_in = [
        local(upper.at[:, pl.ds(g * quarter, quarter)], s["up_in"].at[:, pl.ds(g * quarter, quarter)])
        for g in range(4)
    ]

    recv_ids = {}
    sent = [0]
    row_bytes = n * 2

    def recv_sem(key):
        return s["recv_sem"].at[recv_ids.setdefault(key, len(recv_ids))]

    def remote(src, dst, key, device):
        return pltpu.make_async_remote_copy(
            src_ref=src,
            dst_ref=dst,
            send_sem=s["send_sem"].at[len(sent) - 1],
            recv_sem=recv_sem(key),
            device_id=device,
            device_id_type=MESH,
        )

    def send(key, src, dst, device):
        size = math.prod(src.shape) * 2
        if sent[-1] + size > positions * B * row_bytes:
            sent.append(0)
        sent[-1] += size
        remote(src, dst, key, device).start()

    def arrive(key, dst):
        remote(dst, dst, key, partner).wait_recv()

    def wait_sent():
        for i, size in enumerate(sent):
            every = s["fwd"].at[0, pl.ds(0, size // row_bytes)]
            pltpu.make_async_remote_copy(
                src_ref=every,
                dst_ref=every,
                send_sem=s["send_sem"].at[i],
                recv_sem=s["recv_sem"].at[0],
                device_id=partner,
                device_id_type=MESH,
            ).wait_send()

    for copy in small:
        copy.wait()

    targets = s["target"][...]
    order = lax.broadcasted_iota(jnp.int32, targets.shape, 0)
    before, last = jnp.zeros_like(targets), jnp.zeros_like(targets)
    for e in range(slots):
        row = s["target"][e : e + 1, :]
        before = jnp.where((targets == row) & (order > e), e + 1, before)
        last = jnp.where(row == order, e + 1, last)
    s["table"][:slots, :] = before
    s["table"][slots:, :] = last

    def own_rows(row):
        return pl.ds(pl.multiple_of(row * (2 * B), 2 * B), 2 * B)

    def own_half(row, j):
        return pl.ds(pl.multiple_of(row * (2 * B) + j * B, B), B)

    for j in range(2):
        solved = dot(s["inv_ll"][j], s["rhs_low"][pl.ds(j * B, B)]).astype(BF)
        for k in range(GROUPS):
            s["fwd"][k, own_half(r, j)] = solved[:, k * n : (k + 1) * n]

    pl.semaphore_wait(barrier, len(neighbours))

    s["sum_a"][0] = jnp.zeros((B, B), F32)
    s["sum_b"][0] = jnp.zeros((B, B), F32)

    def build(source, arrivals, starts, write):
        def one(acc, m):
            for e in range(slots):
                before = s["tbl"][e, m]
                acc[e + 1] = source[e, m].astype(F32) + acc[before]

        def put(acc, m):
            for q in range(slots):
                last = s["tbl"][slots + q, m]
                write(q, m, acc[last].astype(BF))

        def step(i, carry):
            m0, m1 = i, i + 1
            one(s["sum_a"], m0)
            one(s["sum_b"], m1)
            put(s["sum_a"], m0)
            put(s["sum_b"], m1)
            return carry

        for arrival, start in zip(arrivals, starts):
            arrival.wait()
            if not table_ready:
                table_in.wait()
                table_ready.append(True)
            for half in range(2):
                lax.fori_loop(0, quarter // 4, lambda i, _: step(start + half * 2 + 2 * i, _), 0)
                yield

    def write_low(q, m, value):
        s["low"][q // RING, q % RING, :, pl.ds(pl.multiple_of(m * B, B), B)] = value

    def write_up(q, m, value):
        s["up"][m, :, pl.ds(q * B, B)] = value

    table_in, table_ready = local(s["table"], s["tbl"]), []
    low_build = build(
        s["low_in"], lower_in, [wrap(y + d) * quarter for d in NEAR_FIRST], write_low
    )
    up_build = build(s["up_in"], upper_in, [g * quarter for g in range(4)], write_up)

    built = [0]

    def low_steps():
        for _ in low_build:
            built[0] += 1
            yield

    low_steps = low_steps()

    def ensure(count):
        while built[0] < count:
            next(low_steps)

    def builds():
        yield from low_steps
        yield from up_build

    building = builds()

    def finish(gen):
        for _ in gen:
            pass

    def group(k):
        fwd, solved = s["fwd"].at[k], s["solved"].at[k]
        acc, low_acc = s["acc"].at[k], s["low_acc"].at[k]

        def row_of(d, side):
            return wrap(y + d) * 2 + (core if side == 0 else 1 - core)

        def low_dot(a, d):
            span = pl.ds(pl.multiple_of(wrap(y + d) * (RING * B), RING * B), RING * B)
            rows = s["low"][a, :, :, span].reshape(RING * B, RING * B)
            part = dot(rows, fwd[span]).reshape(RING, B, n)
            acc[a] = part if d == 0 else acc[a] + part

        def low_dots(d):
            ensure(2 * NEAR_FIRST.index(d) + 2)
            arrive((k, "gc", d), fwd.at[own_rows(row_of(d, 1))])

            def step(a, carry):
                low_dot(a, d)
                return carry

            lax.fori_loop(0, RING, step, 0)

        own = fwd.at[own_rows(r)]
        send((k, "gy", 1), own, own, y_at(1))
        send((k, "gy", -1), own, own, y_at(-1))
        send((k, "gc", 0), own, own, partner)
        yield
        before = fwd.at[own_rows(row_of(-1, 0))]
        arrive((k, "gy", 1), before)
        part = fwd.at[own_half(row_of(-1, 0), 0)]
        send((k, "gy2",), part, part, y_at(1))
        send((k, "gc", -1), before, before, partner)
        after = fwd.at[own_rows(row_of(1, 0))]
        arrive((k, "gy", -1), after)
        part = fwd.at[own_half(row_of(1, 0), 1)]
        send((k, "gy2",), part, part, y_at(-1))
        send((k, "gc", 1), after, after, partner)
        yield
        low_dots(0)
        yield
        low_dots(-1)
        beyond = fwd.at[own_rows(row_of(2, 0))]
        arrive((k, "gy2",), beyond)
        send((k, "gc", 2), beyond, beyond, partner)
        yield
        low_dots(1)
        yield
        ensure(2 * RING)
        arrive((k, "gc", 2), fwd.at[own_rows(row_of(2, 1))])

        at_of = ((x_at, z_at), (z_at, x_at))
        cols = (pl.ds(0, w), pl.ds(w, w))

        def place(f, dh, dl):
            if f == 0:
                return wrap(x + dh), wrap(z + dl)
            return wrap(x + dl), wrap(z + dh)

        def mine(f, dh, dl):
            a, b = place(f, dh, dl)
            return acc[a, b, :, cols[f]]

        def far(f, block):
            for i, sides in enumerate(((2, 1), (-1, 0))):
                for t, dl in enumerate(sides):
                    s["far_s"][k, f, i, t] = block(dl).astype(BF)
                d = 1 - 2 * i
                send(
                    (k, "far", f, d), s["far_s"].at[k, f, i], s["far_r"].at[k, f, i], at_of[f][0](d)
                )

        low_dot(wrap(x + 2), 2)
        far(0, lambda dl: mine(0, 2, dl))

        def rest(i, carry):
            low_dot(wrap(x + i - 1), 2)
            return carry

        lax.fori_loop(0, 3, rest, 0)
        far(1, lambda dl: mine(1, 2, dl))
        for f in range(2):
            for i, sides in enumerate(((-1, 0), (2, 1))):
                d = 1 - 2 * i
                for t, dl in enumerate(sides):
                    s["near_s"][k, f, i, t] = mine(f, d, dl).astype(BF)
                send(
                    (k, "ns", f, 1 - i),
                    s["near_s"].at[k, f, i],
                    s["ns_r"].at[k, f, 1 - i, 0],
                    at_of[f][0](d),
                )
        yield
        sides = ((2, 1), (-1, 0))
        for f in range(2):
            for i in range(2):
                d = 1 - 2 * i
                arrive((k, "far", f, d), s["far_r"].at[k, f, i])
                for t, dl in enumerate(sides[i]):
                    total = mine(f, d, dl) + s["far_r"][k, f, i, t].astype(F32)
                    s["sum_s"][k, f, i, t] = total.astype(BF)
                send(
                    (k, "ns", f, i),
                    s["sum_s"].at[k, f, i],
                    s["ns_r"].at[k, f, i, 1],
                    at_of[f][0](d),
                )
        yield
        for f in range(2):
            for i in range(2):
                arrive((k, "ns", f, i), s["ns_r"].at[k, f, i])
                for t, dl in enumerate(sides[i]):
                    total = mine(f, 0, dl) + s["ns_r"][k, f, i, 0, t].astype(F32)
                    total = total + s["ns_r"][k, f, i, 1, t].astype(F32)
                    if dl == 0:
                        s["lsum"][k, f] = total
                        continue
                    u = LIGHT.index(dl)
                    s["light_s"][k, f, u] = total.astype(BF)
                    send(
                        (k, "light", f),
                        s["light_s"].at[k, f, u],
                        s["light_r"].at[k, f, u],
                        at_of[f][1](dl),
                    )
        yield

        if k == 0:
            for copy in top_in:
                copy.wait()

        def block(f, dh, dl):
            a, b = place(f, dh, dl)
            return solved.at[a, b, :, cols[f]]

        passed = {(0, 1), (-1, -1), (1, 1), (2, -1)}

        def spread(f, dl):
            for d in (1, -1):
                key = (k, "pass", f, dl) if (dl, d) in passed else (k, "rest")
                send(key, block(f, 0, dl), block(f, 0, dl), at_of[f][0](d))

        for f in range(2):
            lsum = s["lsum"][k, f]
            arrive((k, "light", f), s["light_r"].at[k, f])
            for u in range(RING - 1):
                lsum = lsum + s["light_r"][k, f, u].astype(F32)
            rhs = s["rhs_top"][:, k * n + f * w : k * n + (f + 1) * w]
            resid_top = (rhs.astype(F32) - lsum).astype(BF)
            fwd_top = dot(s["inv_lt"][...], resid_top).astype(BF)
            solved[x, z, :, cols[f]] = dot(s["inv_ut"][...], fwd_top).astype(BF)
            for d in (2, 1, -1):
                send((k, "sl", f, d), block(f, 0, 0), block(f, 0, 0), at_of[f][1](d))
            spread(f, 0)
        local_open.append(local(solved.at[x, z], out_top.at[:, pl.ds(k * n, n)]))
        yield
        for d in (1, -1, 2):
            for f in range(2):
                arrive((k, "sl", f, d), block(f, 0, -d if d != 2 else 2))
                spread(f, -d if d != 2 else 2)
        yield

        def relay(f, dl, d):
            arrive((k, "pass", f, dl), block(f, -d, dl))
            send((k, "rest"), block(f, -d, dl), block(f, -d, dl), at_of[f][0](d))

        for dl, d in ((0, 1), (-1, -1), (1, 1)):
            for f in range(2):
                relay(f, dl, d)
        yield
        for f in range(2):
            relay(f, 2, -1)
        yield
        finish(building)
        arrive((k, "rest"), solved.at[pl.ds(0, 2)])

        def pair(d):
            i = d % RING
            first = pl.multiple_of(wrap(y + d) * RING, RING)
            rows = s["up"][pl.ds(first, RING)].reshape(RING * B, -1)
            low_acc[i] = dot(rows, solved[...].reshape(-1, n)).reshape(2, 2, B, n)
            s["pair_s"][k, i] = low_acc[i, 1 - core].astype(BF)
            send((k, "pair", d), s["pair_s"].at[k, i], s["pair_r"].at[k, i], partner)

        def paired(d):
            i = d % RING
            arrive((k, "pair", d), s["pair_r"].at[k, i])
            return low_acc[i, core] + s["pair_r"][k, i].astype(F32)

        for d in (2, 1, -1):
            pair(d)
        value = paired(2)
        for j, d in ((0, 1), (1, -1)):
            s["row_far_s"][k, j] = value[j].astype(BF)
            send((k, "yfar", d), s["row_far_s"].at[k, j], s["row_far_r"].at[k, j], y_at(d))
        pair(0)
        for j, d in ((1, 1), (0, -1)):
            low_acc[d % RING, core] = paired(d)
            s["row_near_s"][k, j] = low_acc[d % RING, core, j].astype(BF)
            send((k, "yns", j), s["row_near_s"].at[k, j], s["row_ns_r"].at[k, j, 0], y_at(d))
        yield
        for j, d in ((0, 1), (1, -1)):
            arrive((k, "yfar", d), s["row_far_r"].at[k, j])
            total = low_acc[d % RING, core, j] + s["row_far_r"][k, j].astype(F32)
            s["row_sum_s"][k, j] = total.astype(BF)
            send((k, "yns", j), s["row_sum_s"].at[k, j], s["row_ns_r"].at[k, j, 1], y_at(d))
        low_acc[0, core] = paired(0)
        yield
        for j in range(2):
            arrive((k, "yns", j), s["row_ns_r"].at[k, j])
            usum = low_acc[0, core, j] + s["row_ns_r"][k, j, 0].astype(F32)
            usum = usum + s["row_ns_r"][k, j, 1].astype(F32)
            resid = (fwd[own_half(r, j)].astype(F32) - usum).astype(BF)
            s["out_low"][k, pl.ds(j * B, B)] = dot(s["inv_ul"][j], resid).astype(BF)
        local_open.append(local(s["out_low"].at[k], out_low.at[:, pl.ds(k * n, n)]))

    live = [(k * LAG, group(k)) for k in range(GROUPS)]
    turn = 0
    while live:
        for item in list(live):
            if turn >= item[0] and next(item[1], "done") == "done":
                live.remove(item)
            next(building, None)
        turn += 1
    for copy in local_open:
        copy.wait()
    wait_sent()


def settle(low, top, out_low, out_top, low_buf, top_buf, sem):
    ins = [
        pltpu.make_async_copy(low, low_buf, sem.at[0]),
        pltpu.make_async_copy(top, top_buf, sem.at[1]),
    ]
    outs = [
        pltpu.make_async_copy(low_buf, out_low, sem.at[2]),
        pltpu.make_async_copy(top_buf, out_top, sem.at[3]),
    ]
    for copy in ins:
        copy.start()
    for before, after in zip(ins, outs):
        before.wait()
        after.start()
    for copy in outs:
        copy.wait()


def body(
    rhs_low,
    rhs_top,
    lower_blocks,
    upper_blocks,
    block_target,
    inv_lower_low,
    inv_upper_low,
    inv_lower_top,
    inv_upper_top,
):
    slots, positions, B, _ = lower_blocks.shape
    count = rhs_low.shape[1]
    C, n = GROUPS, rhs_low.shape[1] // GROUPS
    w = n // 2
    VM = pltpu.VMEM

    scratch = {
        "target": VM(block_target.shape, jnp.int32),
        "table": VM((2 * slots, positions), jnp.int32),
        "tbl": pltpu.SMEM((2 * slots, positions), jnp.int32),
        "rhs_low": VM(rhs_low.shape, BF),
        "inv_ll": VM(inv_lower_low.shape, BF),
        "inv_ul": VM(inv_upper_low.shape, BF),
        "rhs_top": VM((B, count), BF),
        "inv_lt": VM((B, B), BF),
        "inv_ut": VM((B, B), BF),
        "low_in": VM(lower_blocks.shape, BF),
        "up_in": VM(upper_blocks.shape, BF),
        "low": VM((RING, RING, B, positions * B), BF),
        "up": VM((positions, B, RING * RING * B), BF),
        "sum_a": VM((slots + 1, B, B), F32),
        "sum_b": VM((slots + 1, B, B), F32),
        "fwd": VM((C, positions * B, n), BF),
        "solved": VM((C, RING, RING, B, n), BF),
        "acc": VM((C, RING, RING, B, n), F32),
        "lsum": VM((C, 2, B, w), F32),
        "low_acc": VM((C, RING, 2, 2, B, n), F32),
        "pair_s": VM((C, RING, 2, B, n), BF),
        "pair_r": VM((C, RING, 2, B, n), BF),
        "out_low": VM((C, 2 * B, n), BF),
        "light_s": VM((C, 2, RING - 1, B, w), BF),
        "light_r": VM((C, 2, RING - 1, B, w), BF),
        **{t: VM((C, 2, 2, 2, B, w), BF) for t in ("far_s", "far_r", "near_s", "sum_s")},
        "ns_r": VM((C, 2, 2, 2, 2, B, w), BF),
        **{t: VM((C, 2, B, n), BF) for t in ("row_far_s", "row_far_r", "row_near_s", "row_sum_s")},
        "row_ns_r": VM((C, 2, 2, B, n), BF),
        "local_sem": pltpu.SemaphoreType.DMA((16 + 2 * C,)),
        "send_sem": pltpu.SemaphoreType.DMA((5 * C,)),
        "recv_sem": pltpu.SemaphoreType.DMA((40 * C,)),
    }
    anywhere = pl.BlockSpec(memory_space=pl.ANY)
    low, top = pl.pallas_call(
        functools.partial(kernel, tuple(scratch)),
        out_shape=(
            jax.ShapeDtypeStruct((2 * B, count), BF),
            jax.ShapeDtypeStruct((B, count), BF),
        ),
        in_specs=[anywhere] * 9,
        out_specs=(anywhere, anywhere),
        scratch_shapes=list(scratch.values()),
        compiler_params=pltpu.CompilerParams(
            collective_id=0, has_side_effects=True, vmem_limit_bytes=66_000_000
        ),
    )(
        block_target,
        rhs_low,
        rhs_top,
        lower_blocks,
        upper_blocks,
        inv_lower_low,
        inv_upper_low,
        inv_lower_top,
        inv_upper_top,
    )
    return pl.pallas_call(
        settle,
        out_shape=(
            jax.ShapeDtypeStruct(low.shape, BF),
            jax.ShapeDtypeStruct(top.shape, BF),
        ),
        in_specs=[anywhere] * 2,
        out_specs=(anywhere, anywhere),
        scratch_shapes=[
            VM(low.shape, BF),
            VM(top.shape, BF),
            pltpu.SemaphoreType.DMA((4,)),
        ],
    )(low, top)


def solution(mesh):
    placed = (
        P(("row", "col"), None),
        P("row", None),
        P("row", "col", None, None),
        P("row", "col", None, None),
        P("row", "col"),
        P(("row", "col"), None, None),
        P(("row", "col"), None, None),
        P("row", None, None),
        P("row", None, None),
    )
    return jax.shard_map(
        body,
        mesh=mesh,
        in_specs=placed,
        out_specs=(P(("row", "col"), None), P(("row", "col"), None)),
        check_vma=False,
    )
```

time: 83.4 us -> 75.2 us (0.902)
  local copies, waits for them, and re-layouts: 3.9 us -> 0 us
  Pallas kernels: 77.2 us -> 74 us
  other arithmetic: 0.91 us -> 0 us
    pallas_call x1, Pallas kernels: 77.2 us -> 72.2 us  [body(): pl.pallas_call(functools.partial(kernel, tuple(scratch)), out_shape=(jax....]
    unnamed x2 -> x0, local copies, waits for them, and re-layouts: 3.24 us -> none
    pallas_call x0 -> x1, Pallas kernels: none -> 1.73 us  [body(): pl.pallas_call(settle, out_shape=(jax.ShapeDtypeStruct(low.shape, BF), ja...]
    reduce_max x1 -> x0, other arithmetic: 0.89 us -> none  [tables(): before = jnp.max(jnp.where(same & earlier, number, 0), axis=0)]
where the time goes in v2:
time: 75.2 us; the launch traced here: 74.8 us
  Pallas kernels  74 us (98%)
  between operations  0.8 us (1%)
    pallas_call x1, Pallas kernels, body(): pl.pallas_call(functools.partial(kernel, tuple(scratch)), out_shape=(jax....  72.2 us
    pallas_call x1, Pallas kernels, body(): pl.pallas_call(settle, out_shape=(jax.ShapeDtypeStruct(low.shape, BF), ja...  1.73 us

profile of v2, /device:TPU:0, one launch (start us, length us, event | category | flops | bytes accessed | tf_op | source)
XLA Modules:
  0.0 74.8 jit_solution(3403283727161974382)
XLA Ops:
  0.6 72.2 %shard_map.104 = (bf16[256,512]{1,0:T(8,128)(2,1)}, bf16[128,512]{1,0:T(8,128)(2,1)}) custom-call(s32[16,16]{1,0:T(8,128)} %target.1, bf16[256,512]{1,0:T(8,128)(2,1)} %rhs_low.1, bf16[2048,512]{1,0:T(8,128)(2,1)} %rhs_top.1, bf16[16,16,128,128]{3,2,1,0:T(8,128)(2,1)} %lower.1, bf16[16,16,128,128]{3,2,1,0:T(8,128)(2,1)} %upper.1, ...), custom_call_target="tpu_custom_call" | custom-call | tf_op jit(solution)/shard_map/pallas_call | solution.py:526
  72.9 1.7 %shard_map.105 = (bf16[256,512]{1,0:T(8,128)(2,1)}, bf16[128,512]{1,0:T(8,128)(2,1)}) custom-call(bf16[256,512]{1,0:T(8,128)(2,1)} %get-tuple-element.4.low, bf16[128,512]{1,0:T(8,128)(2,1)} %get-tuple-element.5.top), custom_call_target="tpu_custom_call" | custom-call | tf_op jit(solution)/shard_map/pallas_call | solution.py:549

commit v3 on v2

--- a/solution.py
+++ b/solution.py
@@ -11,8 +11,8 @@
 RING = 4
 NEAR_FIRST = (0, -1, 1, 2)
 LIGHT = (1, -1, 2)
+ORDER = "01" + "b" * 8 + "0011" + "0011" + "01" + "01" + "bbb" + "01" + "bbb" + "01" + "bb" + "01" * 7
 GROUPS = 2
-LAG = 0
 BF, F32 = jnp.bfloat16, jnp.float32
 MESH = pl.DeviceIdType.MESH
 
@@ -266,11 +266,11 @@
         low_dots(0)
         yield
         low_dots(-1)
+        low_dots(1)
+        yield
         beyond = fwd.at[own_rows(row_of(2, 0))]
         arrive((k, "gy2",), beyond)
         send((k, "gc", 2), beyond, beyond, partner)
-        yield
-        low_dots(1)
         yield
         ensure(2 * RING)
         arrive((k, "gc", 2), fwd.at[own_rows(row_of(2, 1))])
@@ -363,7 +363,7 @@
 
         def spread(f, dl):
             for d in (1, -1):
-                key = (k, "pass", f, dl) if (dl, d) in passed else (k, "rest")
+                key = (k, "pass", f, dl) if (dl, d) in passed else (k, "keep")
                 send(key, block(f, 0, dl), block(f, 0, dl), at_of[f][0](d))
 
         for f in range(2):
@@ -398,13 +398,34 @@
             relay(f, 2, -1)
         yield
         finish(building)
-        arrive((k, "rest"), solved.at[pl.ds(0, 2)])
+
+        def low_line(i, blocks, first):
+            rows = pl.ds(pl.multiple_of(wrap(y + i) * RING, RING), RING)
+            lhs, rhs = [], []
+            for dx, dz in blocks:
+                a, b = wrap(x + dx), wrap(z + dz)
+                span = pl.ds(pl.multiple_of((a * RING + b) * B, B), B)
+                lhs.append(s["up"][rows, :, span].reshape(RING * B, B))
+                rhs.append(solved[a, b])
+            part = dot(jnp.concatenate(lhs, axis=1), jnp.concatenate(rhs, axis=0))
+            part = part.reshape(2, 2, B, n)
+            low_acc[i] = part if first else low_acc[i] + part
+
+        early = [(dx, dz) for dx in (0, -1, 1) for dz in (0, -1, 1)]
+        late = [(dx, dz) for dx in (0, -1, 1, 2) for dz in (0, -1, 1, 2) if 2 in (dx, dz)]
+        arrive((k, "keep"), solved.at[0])
+
+        def early_line(i, carry):
+            low_line(i, early, True)
+            return carry
+
+        lax.fori_loop(0, RING, early_line, 0)
+        yield
+        arrive((k, "rest"), solved.at[0])
 
         def pair(d):
             i = d % RING
-            first = pl.multiple_of(wrap(y + d) * RING, RING)
-            rows = s["up"][pl.ds(first, RING)].reshape(RING * B, -1)
-            low_acc[i] = dot(rows, solved[...].reshape(-1, n)).reshape(2, 2, B, n)
+            low_line(i, late, False)
             s["pair_s"][k, i] = low_acc[i, 1 - core].astype(BF)
             send((k, "pair", d), s["pair_s"].at[k, i], s["pair_r"].at[k, i], partner)
 
@@ -440,14 +461,9 @@
             s["out_low"][k, pl.ds(j * B, B)] = dot(s["inv_ul"][j], resid).astype(BF)
         local_open.append(local(s["out_low"].at[k], out_low.at[:, pl.ds(k * n, n)]))
 
-    live = [(k * LAG, group(k)) for k in range(GROUPS)]
-    turn = 0
-    while live:
-        for item in list(live):
-            if turn >= item[0] and next(item[1], "done") == "done":
-                live.remove(item)
-            next(building, None)
-        turn += 1
+    steps = {"0": group(0), "1": group(1), "b": building}
+    for token in ORDER:
+        next(steps[token], None)
     for copy in local_open:
         copy.wait()
     wait_sent()
@@ -520,7 +536,7 @@
         "row_ns_r": VM((C, 2, 2, B, n), BF),
         "local_sem": pltpu.SemaphoreType.DMA((16 + 2 * C,)),
         "send_sem": pltpu.SemaphoreType.DMA((5 * C,)),
-        "recv_sem": pltpu.SemaphoreType.DMA((40 * C,)),
+        "recv_sem": pltpu.SemaphoreType.DMA((42 * C,)),
     }
     anywhere = pl.BlockSpec(memory_space=pl.ANY)
     low, top = pl.pallas_call(

time: 75.2 us -> 70 us (0.931)
  Pallas kernels: 74 us -> 68.4 us
    pallas_call x1, Pallas kernels: 72.2 us -> 66.6 us  [body(): pl.pallas_call(functools.partial(kernel, tuple(scratch)), out_shape=(jax....]
where the time goes in v3:
time: 70 us; the launch traced here: 69.2 us
  Pallas kernels  68.4 us (98%)
  between operations  0.8 us (1%)
    pallas_call x1, Pallas kernels, body(): pl.pallas_call(functools.partial(kernel, tuple(scratch)), out_shape=(jax....  66.6 us
    pallas_call x1, Pallas kernels, body(): pl.pallas_call(settle, out_shape=(jax.ShapeDtypeStruct(low.shape, BF), ja...  1.73 us

profile of v3, /device:TPU:0, one launch (start us, length us, event | category | flops | bytes accessed | tf_op | source)
XLA Modules:
  0.0 69.2 jit_solution(9987608024542894037)
XLA Ops:
  0.6 66.6 %shard_map.104 = (bf16[256,512]{1,0:T(8,128)(2,1)}, bf16[128,512]{1,0:T(8,128)(2,1)}) custom-call(s32[16,16]{1,0:T(8,128)} %target.1, bf16[256,512]{1,0:T(8,128)(2,1)} %rhs_low.1, bf16[2048,512]{1,0:T(8,128)(2,1)} %rhs_top.1, bf16[16,16,128,128]{3,2,1,0:T(8,128)(2,1)} %lower.1, bf16[16,16,128,128]{3,2,1,0:T(8,128)(2,1)} %upper.1, ...), custom_call_target="tpu_custom_call" | custom-call | tf_op jit(solution)/shard_map/pallas_call | solution.py:542
  67.3 1.7 %shard_map.105 = (bf16[256,512]{1,0:T(8,128)(2,1)}, bf16[128,512]{1,0:T(8,128)(2,1)}) custom-call(bf16[256,512]{1,0:T(8,128)(2,1)} %get-tuple-element.4.low, bf16[128,512]{1,0:T(8,128)(2,1)} %get-tuple-element.5.top), custom_call_target="tpu_custom_call" | custom-call | tf_op jit(solution)/shard_map/pallas_call | solution.py:565
